TPU v7x, 32 devices: a whole 2x2x4 slice. The times are simulated.
32 devices in a mesh: dp: 4 (over x, core), row: 4 (over z), col: 2 (over y).
Axes of the slice: x: 2, y: 2, z: 4, core: 2. Of those that a mesh axis runs over, the one named last changes fastest.
Arguments:
- hidden_in: float32 [1024, 32768], P('col', ('dp', 'row')), may hold values from -6 to 6
- lengths: int32 [64], P(('dp', 'row')), may hold values from 1 to 512, as said below
- ln1_gain: float32 [1024], P('col'), may hold values from 0.25 to 1.75
- ln1_shift: float32 [1024], P('col'), may hold values from -3 to 3
- w_qkv: bfloat16 [1024, 3072], P('row', 'col'), may hold values from -0.1875 to 0.1875
- bias_q: float32 [1024], P('col'), may hold values from -3 to 3
- bias_v: float32 [1024], P('col'), may hold values from -3 to 3
- w_out: bfloat16 [1024, 1024], P('col', 'row'), may hold values from -0.375 to 0.375
- bias_out: float32 [1024], P('col'), may hold values from -3 to 3
- ln2_gain: float32 [1024], P('col'), may hold values from 0.25 to 1.75
- ln2_shift: float32 [1024], P('col'), may hold values from -3 to 3
- w_up: bfloat16 [1024, 4096], P('row', 'col'), may hold values from -0.1875 to 0.1875
- bias_up: float32 [4096], P('col'), may hold values from -3 to 3
- w_down: bfloat16 [4096, 1024], P('col', 'row'), may hold values from -0.125 to 0.125
- bias_down: float32 [1024], P('col'), may hold values from -3 to 3
- cotangent: float32 [1024, 32768], P('col', ('dp', 'row')), may hold values from -6 to 6
Outputs:
- hidden_out: float32 [1024, 32768], P('col', ('dp', 'row'))
- grad_in: float32 [1024, 32768], P('col', ('dp', 'row'))
- grad_ln1_gain: float32 [1024], P('col')
- grad_ln1_shift: float32 [1024], P('col')
- grad_w_qkv: float32 [1024, 3072], P('row', 'col')
- grad_bias_q: float32 [1024], P('col')
- grad_bias_v: float32 [1024], P('col')
- grad_w_out: float32 [1024, 1024], P('col', 'row')
- grad_bias_out: float32 [1024], P('col')
- grad_ln2_gain: float32 [1024], P('col')
- grad_ln2_shift: float32 [1024], P('col')
- grad_w_up: float32 [1024, 4096], P('row', 'col')
- grad_bias_up: float32 [4096], P('col')
- grad_w_down: float32 [4096, 1024], P('col', 'row')
- grad_bias_down: float32 [1024], P('col')
Inputs may be any that keep to these rules, and one draw needn't show every extreme that they name: `lengths`: each slot holds one sequence of this many tokens followed by padding; some slot of every index pair of dp and row is full.
All inputs are finite; a program needn't handle non-finite values.
Results may differ from a plain program's by a relative error of at most 0.019.
Values may be sent and summed in bfloat16 or wider, within the bound.
A program may use at most 192 MiB of HBM per device.

v0:
```python
from functools import partial
import jax
import jax.numpy as jnp
from jax import lax
from jax.sharding import PartitionSpec as P

HEADS = 16
HEAD = 64
EPS = 1e-05
NEG = -1e30


def norm_forward(value, gain, shift):
    width = value.shape[1] * lax.axis_size("col")
    sums = lax.psum((jnp.sum(value, axis=1), jnp.sum(value * value, axis=1)), "col")
    mean = (sums[0] / width)[:, None]
    var = (sums[1] / width)[:, None] - mean * mean
    inverse = lax.rsqrt(var + EPS)
    normed = (value - mean) * inverse
    return (normed, inverse, (normed * gain + shift).astype(jnp.bfloat16))


def norm_backward(incoming, normed, inverse, gain):
    width = incoming.shape[1] * lax.axis_size("col")
    scaled = incoming * gain
    sums = lax.psum((jnp.sum(scaled, axis=1), jnp.sum(scaled * normed, axis=1)), "col")
    return inverse * (scaled - sums[0][:, None] / width - normed * sums[1][:, None] / width)


def gather_rows(value):
    return lax.all_gather(value, "col", axis=1, tiled=True)


def back_columns(value):
    return lax.psum_scatter(
        value.astype(jnp.bfloat16), "col", scatter_dimension=1, tiled=True
    ).astype(jnp.float32)


def slot_scores(slopes, query, keys, length):
    span = query.shape[0]
    pos = jnp.arange(span)
    offset = (pos[None, :] - pos[:, None]).astype(jnp.float32)
    raw = jnp.einsum("qhd,khd->hqk", query, keys, preferred_element_type=jnp.float32) * 0.125
    raw = raw + slopes[:, None, None] * offset[None]
    visible = (pos[None, :] <= pos[:, None]) & (pos[None, :] < length)
    return jnp.where(visible[None], raw, NEG)


def forward_slot(slopes, item):
    query, keys, values, length = item
    scores = slot_scores(slopes, query, keys, length)
    top = jnp.max(scores, axis=-1, keepdims=True)
    expo = jnp.exp(scores - top)
    total = jnp.sum(expo, axis=-1, keepdims=True)
    probs = expo / total
    attended = jnp.einsum(
        "hqk,khd->qhd", probs.astype(jnp.bfloat16), values, preferred_element_type=jnp.float32
    )
    return (attended, (top + jnp.log(total))[..., 0])


def backward_slot(slopes, item):
    query, keys, values, grad_out, lse, length = item
    scores = slot_scores(slopes, query, keys, length)
    probs = jnp.exp(scores - lse[..., None])
    grad_probs = jnp.einsum("qhd,khd->hqk", grad_out, values, preferred_element_type=jnp.float32)
    grad_values = jnp.einsum(
        "hqk,qhd->khd", probs.astype(jnp.bfloat16), grad_out, preferred_element_type=jnp.float32
    )
    inner = jnp.sum(probs * grad_probs, axis=-1, keepdims=True)
    grad_scores = (probs * (grad_probs - inner)).astype(jnp.bfloat16)
    grad_query = (
        jnp.einsum("hqk,khd->qhd", grad_scores, keys, preferred_element_type=jnp.float32) * 0.125
    )
    grad_keys = (
        jnp.einsum("hqk,qhd->khd", grad_scores, query, preferred_element_type=jnp.float32) * 0.125
    )
    return (grad_query, grad_keys, grad_values)


def body(
    hidden_in,
    lengths,
    ln1_gain,
    ln1_shift,
    w_qkv,
    bias_q,
    bias_v,
    w_out,
    bias_out,
    ln2_gain,
    ln2_shift,
    w_up,
    bias_up,
    w_down,
    bias_down,
    cotangent,
):
    tokens_in = jnp.transpose(hidden_in)
    grad_given = jnp.transpose(cotangent)
    rows = tokens_in.shape[0]
    slots = lengths.shape[0]
    span = rows // slots
    heads_here = w_qkv.shape[1] // (3 * HEAD)
    head_ids = lax.axis_index("col") * heads_here + jnp.arange(heads_here)
    slopes = jnp.exp2(-8.0 * (head_ids.astype(jnp.float32) + 1.0) / HEADS)
    qkv_full, up_full, out_full, down_full = (
        lax.all_gather(w_qkv, "row", axis=0, tiled=True),
        lax.all_gather(w_up, "row", axis=0, tiled=True),
        lax.all_gather(w_out, "row", axis=1, tiled=True),
        lax.all_gather(w_down, "row", axis=1, tiled=True),
    )
    normed1, inverse1, low1 = norm_forward(tokens_in, ln1_gain, ln1_shift)
    rows1 = gather_rows(low1)
    mixed = jnp.dot(rows1, qkv_full, preferred_element_type=jnp.float32).reshape(
        rows, heads_here, 3, HEAD
    )
    query = (
        (mixed[:, :, 0] + bias_q.reshape(heads_here, HEAD))
        .astype(jnp.bfloat16)
        .reshape(slots, span, heads_here, HEAD)
    )
    keys = mixed[:, :, 1].astype(jnp.bfloat16).reshape(slots, span, heads_here, HEAD)
    values = (
        (mixed[:, :, 2] + bias_v.reshape(heads_here, HEAD))
        .astype(jnp.bfloat16)
        .reshape(slots, span, heads_here, HEAD)
    )
    attended, lse = lax.map(partial(forward_slot, slopes), (query, keys, values, lengths))
    attn_low = attended.reshape(rows, heads_here * HEAD).astype(jnp.bfloat16)
    projected = lax.psum_scatter(
        jnp.dot(attn_low, out_full, preferred_element_type=jnp.float32),
        "col",
        scatter_dimension=1,
        tiled=True,
    )
    hidden1 = tokens_in + projected + bias_out
    normed2, inverse2, low2 = norm_forward(hidden1, ln2_gain, ln2_shift)
    rows2 = gather_rows(low2)
    pre = jnp.dot(rows2, up_full, preferred_element_type=jnp.float32) + bias_up
    act, act_pull = jax.vjp(partial(jax.nn.gelu, approximate=True), pre)
    act_low = act.astype(jnp.bfloat16)
    down_terms = jnp.dot(act_low, down_full, preferred_element_type=jnp.float32)
    result = (
        hidden1
        + lax.psum_scatter(
            down_terms.astype(jnp.bfloat16), "col", scatter_dimension=1, tiled=True
        ).astype(jnp.float32)
        + bias_down
    )
    grad_low = grad_given.astype(jnp.bfloat16)
    grad_full = lax.all_gather(grad_low, "col", axis=1, tiled=True)
    grad_down = jnp.einsum("tf,td->fd", act_low, grad_full, preferred_element_type=jnp.float32)
    grad_act = jnp.einsum("td,fd->tf", grad_full, down_full, preferred_element_type=jnp.float32)
    grad_pre = act_pull(grad_act)[0]
    grad_pre_low = grad_pre.astype(jnp.bfloat16)
    grad_up = jnp.einsum("td,tf->df", rows2, grad_pre_low, preferred_element_type=jnp.float32)
    grad_norm2 = back_columns(
        jnp.einsum("tf,df->td", grad_pre_low, up_full, preferred_element_type=jnp.float32)
    )
    grad_hidden1 = grad_given + norm_backward(grad_norm2, normed2, inverse2, ln2_gain)
    branch_low = grad_hidden1.astype(jnp.bfloat16)
    grad_branch = lax.all_gather(branch_low, "col", axis=1, tiled=True)
    grad_outw = jnp.einsum("tc,td->cd", attn_low, grad_branch, preferred_element_type=jnp.float32)
    grad_attn = jnp.einsum(
        "td,cd->tc", grad_branch, out_full, preferred_element_type=jnp.float32
    ).astype(jnp.bfloat16)
    grad_attn = grad_attn.reshape(slots, span, heads_here, HEAD)
    grad_query, grad_keys, grad_values = lax.map(
        partial(backward_slot, slopes), (query, keys, values, grad_attn, lse, lengths)
    )
    stacked = jnp.stack((grad_query, grad_keys, grad_values), axis=3).reshape(
        rows, 3 * heads_here * HEAD
    )
    stacked_low = stacked.astype(jnp.bfloat16)
    grad_qkv = jnp.einsum("td,tc->dc", rows1, stacked_low, preferred_element_type=jnp.float32)
    grad_norm1 = back_columns(
        jnp.einsum("tc,dc->td", stacked_low, qkv_full, preferred_element_type=jnp.float32)
    )
    grad_input = grad_hidden1 + norm_backward(grad_norm1, normed1, inverse1, ln1_gain)
    small = lax.psum(
        (
            jnp.sum(grad_norm1 * normed1, axis=0),
            jnp.sum(grad_norm1, axis=0),
            jnp.sum(grad_query.reshape(rows, heads_here * HEAD), axis=0),
            jnp.sum(grad_values.reshape(rows, heads_here * HEAD), axis=0),
            jnp.sum(grad_hidden1, axis=0),
            jnp.sum(grad_norm2 * normed2, axis=0),
            jnp.sum(grad_norm2, axis=0),
            jnp.sum(grad_pre, axis=0),
            jnp.sum(grad_given, axis=0),
        ),
        ("dp", "row"),
    )
    local = (grad_qkv, grad_up, grad_outw, grad_down)
    whole = (
        lax.psum(local[0].astype(jnp.bfloat16), "dp").astype(jnp.float32),
        lax.psum(local[1].astype(jnp.bfloat16), "dp").astype(jnp.float32),
        lax.psum(local[2].astype(jnp.bfloat16), "dp").astype(jnp.float32),
        lax.psum(local[3].astype(jnp.bfloat16), "dp").astype(jnp.float32),
    )
    summed = (
        lax.psum_scatter(
            whole[0].astype(jnp.bfloat16), "row", scatter_dimension=0, tiled=True
        ).astype(jnp.float32),
        lax.psum_scatter(
            whole[1].astype(jnp.bfloat16), "row", scatter_dimension=0, tiled=True
        ).astype(jnp.float32),
        lax.psum_scatter(
            whole[2].astype(jnp.bfloat16), "row", scatter_dimension=1, tiled=True
        ).astype(jnp.float32),
        lax.psum_scatter(
            whole[3].astype(jnp.bfloat16), "row", scatter_dimension=1, tiled=True
        ).astype(jnp.float32),
    )
    return (
        jnp.transpose(result),
        jnp.transpose(grad_input),
        small[0],
        small[1],
        summed[0],
        small[2],
        small[3],
        summed[2],
        small[4],
        small[5],
        small[6],
        summed[1],
        small[7],
        summed[3],
        small[8],
    )


def solution(mesh):
    return jax.shard_map(
        body,
        mesh=mesh,
        in_specs=(
            P("col", ("dp", "row")),
            P(("dp", "row")),
            P("col"),
            P("col"),
            P("row", "col"),
            P("col"),
            P("col"),
            P("col", "row"),
            P("col"),
            P("col"),
            P("col"),
            P("row", "col"),
            P("col"),
            P("col", "row"),
            P("col"),
            P("col", ("dp", "row")),
        ),
        out_specs=(
            P("col", ("dp", "row")),
            P("col", ("dp", "row")),
            P("col"),
            P("col"),
            P("row", "col"),
            P("col"),
            P("col"),
            P("col", "row"),
            P("col"),
            P("col"),
            P("col"),
            P("row", "col"),
            P("col"),
            P("col", "row"),
            P("col"),
        ),
        check_vma=False,
    )
```

profile of v0, /device:TPU:0, one launch (start us, length us, event | category | flops | bytes accessed | tf_op | source)
XLA Modules:
  0.0 1329.2 jit_solution(10266186835196599832)
XLA Ops:
  17.6 9.6 all-reduce.4
  34.8 53.8 %all-gather.9.cloned.1.call-done = bf16[2048,1024]{1,0:T(8,128)(2,1)} async-done(((bf16[2048,512]{1,0:T(8,128)(2,1)}), bf16[2048,1024]{1,0:T(8,128)(2,1)}) %all-gather.9.cloned.1.call-update) | async-done | bytes 4194320 | tf_op jit(solution)/shard_map/all_gather | solution.py:31
  88.6 65.1 %all-gather.11.cloned.1.call-done = bf16[1024,1536]{1,0:T(8,128)(2,1)} async-done(((bf16[256,1536]{1,0:T(8,128)(2,1)}), bf16[1024,1536]{1,0:T(8,128)(2,1)}) %all-gather.11.cloned.1.call-update) | async-done | bytes 3145744 | tf_op jit(solution)/shard_map/all_gather | solution.py:109
  153.7 9.8 fusion.100
  169.0 6.1 squeeze.40
  178.3 6.0 squeeze.39
  198.4 53.5 %while.30 = (s32[]{:T(128)}, bf16[4,512,8,64]{1,3,2,0:T(8,128)(2,1)}, f32[4,8,512]{2,1,0:T(8,128)}, bf16[4,512,8,64]{1,3,2,0:T(8,128)(2,1)}, s32[4]{0:T(128)S(1)...) while((s32[]{:T(128)}, ...), condition=%wide.region_7.8_spmd.clone.clone, body=%wide.region_4.7_spmd.clone.sunk.clone | while | flops 575664640 | bytes 49942764 | solution.py:130
  257.8 7.5 fusion.101
  266.0 97.4 %reduce-scatter.9.cloned.1.call-done = f32[2048,512]{1,0:T(8,128)} async-done(((f32[2048,1024]{1,0:T(8,128)}), f32[2048,512]{1,0:T(8,128)}) %reduce-scatter.9.cloned.1.call-update) | async-done | bytes 4194320 | tf_op jit(solution)/shard_map/reduce_scatter | solution.py:132
  363.3 5.9 fusion.90
  369.3 6.9 all-reduce.3
  390.2 55.4 %all-gather.17.cloned.1.call-done = bf16[1024,2048]{1,0:T(8,128)(2,1)} async-done(((bf16[256,2048]{1,0:T(8,128)(2,1)}), bf16[1024,2048]{1,0:T(8,128)(2,1)}) %all-gather.17.cloned.1.call-update) | async-done | bytes 4194320 | tf_op jit(solution)/shard_map/all_gather | solution.py:110
  445.6 56.8 %all-gather.15.cloned.1.call-done = bf16[2048,1024]{1,0:T(8,128)(2,1)} async-done(((bf16[2048,512]{1,0:T(8,128)(2,1)}), bf16[2048,1024]{1,0:T(8,128)(2,1)}) %all-gather.15.cloned.1.call-update) | async-done | bytes 4194320 | tf_op jit(solution)/shard_map/all_gather | solution.py:31
  502.4 15.3 %fusion.102 = f32[2048,2048]{1,0:T(8,128)} fusion(bf16[2048,1024]{1,0:T(8,128)(2,1)} %all-gather.15.cloned.1.call-done, bf16[1024,2048]{1,0:T(8,128)(2,1)} %all-gather.17.cloned.1.call-done), kind=kOutput, calls=%fused_computation.144 | convolution fusion | flops 8589934592 | bytes 25165824 | tf_op jit(solution)/shard_map/dot_general | solution.py:141
  517.7 43.1 %all-gather.21.cloned.1.call-done = bf16[2048,1024]{1,0:T(8,128)(2,1)} async-done(((bf16[2048,512]{1,0:T(8,128)(2,1)}), bf16[2048,1024]{1,0:T(8,128)(2,1)}) %all-gather.21.cloned.1.call-update) | async-done | bytes 4194320 | tf_op jit(solution)/shard_map/all_gather | solution.py:153
  560.8 82.2 %all-gather.19.cloned.1.call-done = bf16[2048,1024]{1,0:T(8,128)(2,1)} async-done(((bf16[2048,256]{1,0:T(8,128)(2,1)}), bf16[2048,1024]{1,0:T(8,128)(2,1)}) %all-gather.19.cloned.1.call-update) | async-done | bytes 4194320 | tf_op jit(solution)/shard_map/all_gather | solution.py:112
  643.0 27.5 %fusion.91 = (f32[2048]{0:T(1024)}, bf16[2048,2048]{1,0:T(8,128)(2,1)}, bf16[2048,2048]{1,0:T(8,128)(2,1)}) fusion(f32[2048,2048]{1,0:T(8,128)} %fusion.102, f32[2048]{0:T(1024)S(1)} %copy-done.34, bf16[2048,1024]{1,0:T(8,128)(2,1)} %all-gather.21.cloned.1.call-done, bf16[2048,1024]{1,0:T(8,128)(2,1)} %all-gather.19.cloned.1.call-done), kind=kOutput, calls=%fused_computation.136 | convolution fusion | flops 8690595840 | bytes 41959424 | tf_op jit(solution)/shard_map/td,fd->tf/dot_general | solution.py:155
  670.5 13.0 fusion.84
  683.6 13.8 %convolution_convert_fusion.2 = bf16[2048,1024]{1,0:T(8,128)(2,1)} fusion(bf16[2048,2048]{1,0:T(8,128)(2,1)} %get-tuple-element.304, bf16[2048,1024]{1,0:T(8,128)(2,1)} %all-gather.19.cloned.1.call-done), kind=kOutput, calls=%fused_computation.122 | convolution fusion | flops 8592031744 | bytes 16777216 | tf_op jit(solution)/shard_map/dot_general | solution.py:144
  697.4 38.7 %reduce-scatter.13.cloned.1.call-done = bf16[2048,512]{1,0:T(8,128)(2,1)} async-done(((bf16[2048,1024]{1,0:T(8,128)(2,1)}), bf16[2048,512]{1,0:T(8,128)(2,1)}) %reduce-scatter.13.cloned.1.call-update) | async-done | bytes 2097168 | tf_op jit(solution)/shard_map/reduce_scatter | solution.py:35
  741.0 6.9 all-reduce.2
  747.9 44.8 %reduce-scatter.11.cloned.1.call-done = bf16[2048,512]{1,0:T(8,128)(2,1)} async-done(((bf16[2048,1024]{1,0:T(8,128)(2,1)}), bf16[2048,512]{1,0:T(8,128)(2,1)}) %reduce-scatter.11.cloned.1.call-update) | async-done | bytes 2097168 | tf_op jit(solution)/shard_map/reduce_scatter | solution.py:147
  792.8 8.2 fusion.93
  804.6 14.2 %convolution_convert_fusion.3 = bf16[2048,1024]{1,0:T(8,128)(2,1)} fusion(bf16[2048,2048]{1,0:T(8,128)(2,1)} %get-tuple-element.304, bf16[2048,1024]{1,0:T(8,128)(2,1)} %all-gather.21.cloned.1.call-done), kind=kOutput, calls=%fused_computation.123 | convolution fusion | flops 8592031744 | bytes 16777216 | tf_op jit(solution)/shard_map/tf,td->fd/dot_general | solution.py:154
  818.8 14.1 %fusion.87 = bf16[1024,2048]{1,0:T(8,128)(2,1)} fusion(bf16[2048,1024]{1,0:T(8,128)(2,1)} %all-gather.15.cloned.1.call-done, bf16[2048,2048]{1,0:T(8,128)(2,1)} %get-tuple-element.296), kind=kOutput, calls=%fused_computation.121 | convolution fusion | flops 8592031744 | bytes 16777216 | tf_op jit(solution)/shard_map/td,tf->df/dot_general | solution.py:158
  833.0 28.5 %all-gather.23.cloned.1.call-done = bf16[2048,1024]{1,0:T(8,128)(2,1)} async-done(((bf16[2048,512]{1,0:T(8,128)(2,1)}), bf16[2048,1024]{1,0:T(8,128)(2,1)}) %all-gather.23.cloned.1.call-update) | async-done | bytes 4194320 | tf_op jit(solution)/shard_map/all_gather | solution.py:164
  874.6 6.1 convolution_convert_fusion.5
  880.7 133.4 %while.31 = (s32[]{:T(128)}, f32[4,512,8,64]{1,3,2,0:T(8,128)}, bf16[4,512,8,64]{1,3,2,0:T(8,128)(2,1)}, f32[4,512,8,64]{1,3,2,0:T(8,128)}, bf16[4,512,8,64]{1,3...) while((s32[]{:T(128)}, f32[4,512,8,64]{1,3,2,0:T(8,128)}, ...), condition=%wide.region_21.22_spmd.clone.clone, body=%wide.region_19.21_spmd.clone.sunk.clone | while | flops 1366815232 | bytes 122771752 | solution.py:170
  885.3 8.9 multiply_reduce_fusion.4
  894.2 8.1 multiply_convert_fusion.4
  902.4 6.1 fusion.182
  918.7 8.9 multiply_reduce_fusion.4
  927.6 8.1 multiply_convert_fusion.4
  952.0 8.9 multiply_reduce_fusion.4
  960.9 8.1 multiply_convert_fusion.4
  969.1 6.0 fusion.182
  985.3 8.9 multiply_reduce_fusion.4
  994.3 8.1 multiply_convert_fusion.4
  1002.4 6.0 fusion.182
  1014.6 7.1 fusion.97
  1022.4 8.3 copy.58
  1039.0 8.4 convolution_convert_fusion
  1050.7 61.7 %reduce-scatter.17.cloned.1.call-done = bf16[256,1536]{1,0:T(8,128)(2,1)} async-done(((bf16[1024,1536]{1,0:T(8,128)(2,1)}), bf16[256,1536]{1,0:T(8,128)(2,1)}) %reduce-scatter.17.cloned.1.call-update) | async-done | bytes 786448 | tf_op jit(solution)/shard_map/reduce_scatter | solution.py:204
  1112.4 11.7 convolution_convert_fusion.1
  1132.2 51.7 %all-reduce.8.cloned.1.call-done = (bf16[256,1536]{1,0:T(8,128)(2,1)}, bf16[512,256]{1,0:T(8,128)(2,1)}, bf16[256,2048]{1,0:T(8,128)(2,1)}, bf16[2048,256]{1,0:T(8,128)(2,1)}) async-done(((bf16[256,1536]{1,0:T(8,128)(2,1)}, bf16[512,256]{1,0:T(8,128)(2,1)}, bf16[256,2048]{1,0:T(8,128)(2,1)}, bf16[2048,256]{1,0:T(8,128)(2,1)}), (bf16[256,1536]{1,0:T(8,128)(2,1)}, bf16[512,256]{1,0:T(8,128)(2,1)}, ...) | async-done | bytes 3145744 | tf_op jit(solution)/shard_map/psum | solution.py:198
  1192.5 47.9 %reduce-scatter.15.cloned.1.call-done = bf16[2048,512]{1,0:T(8,128)(2,1)} async-done(((bf16[2048,1024]{1,0:T(8,128)(2,1)}), bf16[2048,512]{1,0:T(8,128)(2,1)}) %reduce-scatter.15.cloned.1.call-update) | async-done | bytes 2097168 | tf_op jit(solution)/shard_map/reduce_scatter | solution.py:35
  1244.7 6.9 all-reduce.1
  1262.6 59.9 %all-reduce = (f32[512]{0:T(512)}, f32[512]{0:T(512)}, f32[512]{0:T(512)}, f32[512]{0:T(512)}, f32[512]{0:T(512)}, /*index=5*/f32[512]{0:T(512)}, f32[512]{0:T(512)}, f32[2048]{0:T(1024)}, f32[512]{0:T(512)}) all-reduce(f32[512]{0:T(512)S(1)} %get-tuple-element.228, ...), channel_id=1, replica_groups=mesh['dp'=4,'row'=4,'col'=2] {'dp','row'}, use_global_device_ids=true, to_apply=%region_28.29 | all-reduce | flops 6144 | bytes 49152 | tf_op jit(solution)/shard_map/psum | solution.py:182
  (262 shorter events, 227.5 us)
Async XLA Ops:
  7.2 81.4 %all-gather.9.cloned.1.call-start = ((), (), s32[]{:S(2)}) async-start(), calls=%async_computation.8 | async-start | bytes 6291456 | tf_op jit(solution)/shard_map/all_gather | solution.py:31
  12.6 15.2 %copy-start.19 = (f32[512]{0:T(512)S(1)}, f32[512]{0:T(512)}, u32[]{:S(2)}) copy-start(f32[512]{0:T(512)} %param.22) | copy-start | bytes 6148
  12.6 15.2 %copy-start.25 = (f32[512]{0:T(512)S(1)}, f32[512]{0:T(512)}, u32[]{:S(2)}) copy-start(f32[512]{0:T(512)} %param.23) | copy-start | bytes 6148
  31.4 122.2 %all-gather.11.cloned.1.call-start = ((), (), s32[]{:S(2)}) async-start(), calls=%async_computation.9 | async-start | bytes 3932160 | tf_op jit(solution)/shard_map/all_gather | solution.py:109
  32.2 225.6 %all-gather.13.cloned.1.call-start = ((), (), s32[]{:S(2)}) async-start(), calls=%async_computation.10 | async-start | bytes 1310720 | tf_op jit(solution)/shard_map/all_gather | solution.py:111
  32.9 330.4 %reduce-scatter.9.cloned.1.call-start = ((), (), s32[]{:S(2)}) async-start(), calls=%async_computation.11 | async-start | bytes 12582912 | tf_op jit(solution)/shard_map/reduce_scatter | solution.py:132
  33.2 130.3 %copy-start.3 = (bf16[4,512,8,64]{1,3,2,0:T(8,128)(2,1)}, bf16[4,512,8,64]{1,3,2,0:T(8,128)(2,1)S(1)}, u32[]{:S(2)}) copy-start(bf16[4,512,8,64]{1,3,2,0:T(8,128)(2,1)S(1)} %fusion.99) | copy-start | bytes 6291460
  190.4 8.0 copy-start.35
  251.9 5.9 copy-start.2
  265.3 98.1 %copy-start.30 = (f32[512]{0:T(512)S(1)}, f32[512]{0:T(512)}, u32[]{:S(2)}) copy-start(f32[512]{0:T(512)} %param.28) | copy-start | bytes 6148
  265.3 180.3 %all-gather.17.cloned.1.call-start = ((), (), s32[]{:S(2)}) async-start(), calls=%async_computation.13 | async-start | bytes 5242880 | tf_op jit(solution)/shard_map/all_gather | solution.py:110
  265.9 110.3 %copy-start.18 = (f32[512]{0:T(512)S(1)}, f32[512]{0:T(512)}, u32[]{:S(2)}) copy-start(f32[512]{0:T(512)} %param.29) | copy-start | bytes 6148
  265.9 110.3 %copy-start.26 = (f32[512]{0:T(512)S(1)}, f32[512]{0:T(512)}, u32[]{:S(2)}) copy-start(f32[512]{0:T(512)} %param.30) | copy-start | bytes 6148
  265.9 236.5 %all-gather.15.cloned.1.call-start = ((), (), s32[]{:S(2)}) async-start(), calls=%async_computation.12 | async-start | bytes 6291456 | tf_op jit(solution)/shard_map/all_gather | solution.py:31
  379.9 180.9 %all-gather.21.cloned.1.call-start = ((), (), s32[]{:S(2)}) async-start(), calls=%async_computation.16 | async-start | bytes 6291456 | tf_op jit(solution)/shard_map/all_gather | solution.py:153
  389.4 253.6 %all-gather.19.cloned.1.call-start = ((), (), s32[]{:S(2)}) async-start(), calls=%async_computation.14 | async-start | bytes 5242880 | tf_op jit(solution)/shard_map/all_gather | solution.py:112
  390.2 252.9 %copy-start.34 = (f32[2048]{0:T(1024)S(1)}, f32[2048]{0:T(1024)}, u32[]{:S(2)}) copy-start(f32[2048]{0:T(1024)} %param.32) | copy-start | bytes 24580
  390.2 346.0 %reduce-scatter.13.cloned.1.call-start = ((), (), s32[]{:S(2)}) async-start(), calls=%async_computation.17 | async-start | bytes 6291456 | tf_op jit(solution)/shard_map/reduce_scatter | solution.py:35
  643.0 27.5 %copy-start.32 = (bf16[1024,2048]{1,0:T(8,128)(2,1)S(1)}, bf16[1024,2048]{1,0:T(8,128)(2,1)}, u32[]{:S(2)}) copy-start(bf16[1024,2048]{1,0:T(8,128)(2,1)} %all-gather.17.cloned.1.call-done) | copy-start | bytes 12582916
  683.5 109.2 %reduce-scatter.11.cloned.1.call-start = ((), (), s32[]{:S(2)}) async-start(), calls=%async_computation.15 | async-start | bytes 6291456 | tf_op jit(solution)/shard_map/reduce_scatter | solution.py:147
  697.4 95.4 %copy-start.27 = (f32[512]{0:T(512)S(1)}, f32[512]{0:T(512)}, u32[]{:S(2)}) copy-start(f32[512]{0:T(512)} %param.34) | copy-start | bytes 6148
  697.4 164.1 %all-gather.23.cloned.1.call-start = ((), (), s32[]{:S(2)}) async-start(), calls=%async_computation.18 | async-start | bytes 6291456 | tf_op jit(solution)/shard_map/all_gather | solution.py:164
  736.2 56.6 %copy-start.7 = (bf16[2048,512]{1,0:T(8,128)(2,1)S(1)}, bf16[2048,512]{1,0:T(8,128)(2,1)}, u32[]{:S(2)}) copy-start(bf16[2048,512]{1,0:T(8,128)(2,1)} %reduce-scatter.13.cloned.1.call-done) | copy-start | bytes 6291460
  804.5 242.9 %reduce-scatter.23.cloned.1.call-start = ((), (), s32[]{:S(2)}) async-start(), calls=%async_computation.23 | async-start | bytes 5242880 | tf_op jit(solution)/shard_map/reduce_scatter | solution.py:213
  818.8 228.7 %reduce-scatter.21.cloned.1.call-start = ((), (), s32[]{:S(2)}) async-start(), calls=%async_computation.22 | async-start | bytes 5242880 | tf_op jit(solution)/shard_map/reduce_scatter | solution.py:207
  832.9 28.6 %copy-start.33 = (bf16[512,1024]{1,0:T(8,128)(2,1)S(1)}, bf16[512,1024]{1,0:T(8,128)(2,1)}, u32[]{:S(2)}) copy-start(bf16[512,1024]{1,0:T(8,128)(2,1)} %all-gather.13.cloned.1.call-done) | copy-start | bytes 3145732
  832.9 217.7 %reduce-scatter.19.cloned.1.call-start = ((), (), s32[]{:S(2)}) async-start(), calls=%async_computation.21 | async-start | bytes 1310720 | tf_op jit(solution)/shard_map/reduce_scatter | solution.py:210
  874.6 6.1 copy-start.36
  885.3 8.9 copy-start
  902.4 6.1 copy-start.4
  918.7 8.9 copy-start
  935.8 5.9 copy-start.4
  952.0 8.9 copy-start
  969.1 6.0 copy-start.4
  985.3 8.9 copy-start
  1002.4 6.0 copy-start.4
  1014.1 98.2 %reduce-scatter.17.cloned.1.call-start = ((), (), s32[]{:S(2)}) async-start(), calls=%async_computation.20 | async-start | bytes 3932160 | tf_op jit(solution)/shard_map/reduce_scatter | solution.py:204
  1014.5 7.1 copy-start.6
  1030.7 8.3 copy-start.31
  1047.4 136.4 %all-reduce.8.cloned.1.call-start = ((), (), s32[]{:S(2)}) async-start(), calls=%async_computation.24 | async-start | bytes 6291456 | tf_op jit(solution)/shard_map/psum | solution.py:198
  1112.4 128.0 %reduce-scatter.15.cloned.1.call-start = ((), (), s32[]{:S(2)}) async-start(), calls=%async_computation.19 | async-start | bytes 6291456 | tf_op jit(solution)/shard_map/reduce_scatter | solution.py:35
  1183.8 7.2 copy-start.13
  1185.7 54.7 %copy-start.15 = (f32[2048]{0:T(1024)S(1)}, f32[2048]{0:T(1024)}, u32[]{:S(2)}) copy-start(f32[2048]{0:T(1024)} %copy-done.14) | copy-start | bytes 24580
  1185.7 54.7 %copy-start.17 = (f32[2048]{0:T(1024)S(1)}, f32[2048]{0:T(1024)}, u32[]{:S(2)}) copy-start(f32[2048]{0:T(1024)} %copy-done.16) | copy-start | bytes 24580
  1185.7 54.7 %copy-start.20 = (f32[512]{0:T(512)S(1)}, f32[512]{0:T(512)}, u32[]{:S(2)}) copy-start(f32[512]{0:T(512)} %param.22) | copy-start | bytes 6148
  1240.4 11.2 copy-start.8
  1257.2 5.4 copy-start.23
  1257.2 5.4 copy-start.24
  (21 other events, 52.8 us)
Sparse Core Ops, SparseCore 0:
  31.5 56.9 all-gather.8
  90.1 63.4 all-gather.10
  155.2 28.8 all-gather.12
  265.4 97.8 reduce-scatter.8
  364.8 80.7 all-gather.16
  447.1 55.2 all-gather.14
  504.0 56.7 all-gather.20
  562.4 80.5 all-gather.18
  683.6 52.4 reduce-scatter.12
  738.3 54.3 reduce-scatter.10
  804.7 56.8 all-gather.22
  863.8 76.7 reduce-scatter.22
  942.8 77.3 reduce-scatter.20
  1023.0 27.6 reduce-scatter.18
  1053.4 58.8 reduce-scatter.16
  1114.8 68.9 all-reduce.7
  1186.0 54.3 reduce-scatter.14
where the time goes:
time: 1340 us; the launch traced here: 1330 us
  waiting for transfers between devices  733 us (55%)
  matrix products  269 us (20%)
  other arithmetic  124 us (9%)
  local copies, waits for them, and re-layouts  96.6 us (7%)
  blocking collectives  90.2 us (7%)
  between operations  14.5 us (1%)
    all_gather x2, waiting for transfers between devices, gather_rows(): return lax.all_gather(value, 'col', axis=1, tiled=True)  111 us
    reduce_scatter x1, waiting for transfers between devices, body(): lax.psum_scatter(jnp.dot(attn_low, out_full, preferred_element_type=jnp.f...  97.4 us
    reduce_scatter x2, waiting for transfers between devices, back_columns(): lax.psum_scatter(value.astype(jnp.bfloat16), 'col', scatter_dimension=1,...  86.7 us
    all_gather x1, waiting for transfers between devices, body(): lax.all_gather(w_down, 'row', axis=1, tiled=True)  82.2 us
    all_gather x1, waiting for transfers between devices, body(): lax.all_gather(w_qkv, 'row', axis=0, tiled=True)  65.1 us
    reduce_scatter x1, waiting for transfers between devices, body(): lax.psum_scatter(whole[0].astype(jnp.bfloat16), 'row', scatter_dimension=...  61.7 us
    psum x1, blocking collectives, body(): lax.psum((jnp.sum(grad_norm1 * normed1, axis=0), jnp.sum(grad_norm1, axis...  59.9 us
    all_gather x1, waiting for transfers between devices, body(): lax.all_gather(w_up, 'row', axis=0, tiled=True)  55.4 us
  transfers between devices with their start and end apart: 17, of which 14 were waited for; matrix products, arithmetic and copies ran while one was open for 30% of the time, Pallas kernels for 0%

commit v1 on v0

--- a/solution.py
+++ b/solution.py
@@ -8,6 +8,28 @@
 HEAD = 64
 EPS = 1e-05
 NEG = -1e30
+
+
+def plan_ladders(u_in, out_dim):
+    d_next = list(u_in.shape[1:])
+    d_next[out_dim] *= u_in.shape[0]
+    r_now = jnp.moveaxis(u_in, 0, out_dim).reshape(d_next)
+    return r_now
+
+
+def chunk_order(m, which_axis):
+    p_next, low = (lax.psum(1, axis_name=which_axis), lax.axis_index(which_axis))
+    ready, m_next = (m[None], 1)
+    while m_next < p_next:
+        before = lax.ppermute(
+            ready, axis_name=which_axis, perm=list(map(lambda j: (j, j ^ m_next), range(p_next)))
+        )
+        local_next = low & m_next == 0
+        ready = jnp.concatenate(
+            [jnp.where(local_next, ready, before), jnp.where(local_next, before, ready)]
+        )
+        m_next *= 2
+    return ready
 
 
 def norm_forward(value, gain, shift):
@@ -105,11 +127,17 @@
     heads_here = w_qkv.shape[1] // (3 * HEAD)
     head_ids = lax.axis_index("col") * heads_here + jnp.arange(heads_here)
     slopes = jnp.exp2(-8.0 * (head_ids.astype(jnp.float32) + 1.0) / HEADS)
+
+    def fit_halves(panel, arr_in, dim_no):
+        y2 = chunk_order(panel, arr_in)
+        piece_now = plan_ladders(y2, dim_no)
+        return piece_now
+
     qkv_full, up_full, out_full, down_full = (
         lax.all_gather(w_qkv, "row", axis=0, tiled=True),
         lax.all_gather(w_up, "row", axis=0, tiled=True),
         lax.all_gather(w_out, "row", axis=1, tiled=True),
-        lax.all_gather(w_down, "row", axis=1, tiled=True),
+        fit_halves(w_down, "row", 1),
     )
     normed1, inverse1, low1 = norm_forward(tokens_in, ln1_gain, ln1_shift)
     rows1 = gather_rows(low1)

time: 1340 us -> 1280 us (0.955)
  waiting for transfers between devices: 733 us -> 656 us
    ppermute x0 -> x2, waiting for transfers between devices: none -> 160 us  [chunk_order(): lax.ppermute(ready, axis_name=which_axis, perm=list(map(lambda j: (j, j ^...]
    all_gather x1 -> x0, waiting for transfers between devices: 82.2 us -> none  [body(): lax.all_gather(w_down, 'row', axis=1, tiled=True)]
    all_gather x2, waiting for transfers between devices: 111 us -> 53.8 us  [gather_rows(): return lax.all_gather(value, 'col', axis=1, tiled=True)]
    all_gather x1, waiting for transfers between devices: 55.4 us -> 0.01 us  [body(): lax.all_gather(w_up, 'row', axis=0, tiled=True)]
    all_gather x1, waiting for transfers between devices: 43.1 us -> 0.01 us  [body(): grad_full = lax.all_gather(grad_low, 'col', axis=1, tiled=True)]
    dot_general x1, matrix products: 15.3 us -> 29.2 us  [body(): pre = jnp.dot(rows2, up_full, preferred_element_type=jnp.float32) + bias_up]
    unnamed x76 -> x81, local copies, waits for them, and re-layouts: 47.8 us -> 51.5 us
  transfers between devices with their start and end apart: 17 -> 18, of which waited for: 14 -> 12; matrix products, arithmetic and copies ran while one was open for 30% -> 33% of each run, Pallas kernels for 0% -> 0%
where the time goes in v1:
time: 1280 us; the launch traced here: 1270 us
  waiting for transfers between devices  656 us (51%)
  matrix products  278 us (22%)
  other arithmetic  131 us (10%)
  local copies, waits for them, and re-layouts  100 us (8%)
  blocking collectives  90.2 us (7%)
  between operations  14.8 us (1%)
    ppermute x2, waiting for transfers between devices, chunk_order(): lax.ppermute(ready, axis_name=which_axis, perm=list(map(lambda j: (j, j ^...  160 us
    reduce_scatter x1, waiting for transfers between devices, body(): lax.psum_scatter(jnp.dot(attn_low, out_full, preferred_element_type=jnp.f...  97.4 us
    reduce_scatter x2, waiting for transfers between devices, back_columns(): lax.psum_scatter(value.astype(jnp.bfloat16), 'col', scatter_dimension=1,...  87.6 us
    all_gather x1, waiting for transfers between devices, body(): lax.all_gather(w_qkv, 'row', axis=0, tiled=True)  65.1 us
    reduce_scatter x1, waiting for transfers between devices, body(): lax.psum_scatter(whole[0].astype(jnp.bfloat16), 'row', scatter_dimension=...  61.7 us
    psum x1, blocking collectives, body(): lax.psum((jnp.sum(grad_norm1 * normed1, axis=0), jnp.sum(grad_norm1, axis...  59.9 us
    all_gather x2, waiting for transfers between devices, gather_rows(): return lax.all_gather(value, 'col', axis=1, tiled=True)  53.8 us
    psum x1, waiting for transfers between devices, body(): lax.psum(local[0].astype(jnp.bfloat16), 'dp').astype(jnp.float32)  51.6 us
  transfers between devices with their start and end apart: 18, of which 12 were waited for; matrix products, arithmetic and copies ran while one was open for 33% of the time, Pallas kernels for 0%

profile of v1, /device:TPU:0, one launch (start us, length us, event | category | flops | bytes accessed | tf_op | source)
XLA Modules:
  0.0 1274.0 jit_solution(15654692455420734214)
XLA Ops:
  17.6 9.6 all-reduce.4
  34.8 53.8 %all-gather.8.cloned.1.call-done = bf16[2048,1024]{1,0:T(8,128)(2,1)} async-done(((bf16[2048,512]{1,0:T(8,128)(2,1)}), bf16[2048,1024]{1,0:T(8,128)(2,1)}) %all-gather.8.cloned.1.call-update) | async-done | bytes 4194320 | tf_op jit(solution)/shard_map/all_gather | solution.py:53
  88.6 65.1 %all-gather.10.cloned.1.call-done = bf16[1024,1536]{1,0:T(8,128)(2,1)} async-done(((bf16[256,1536]{1,0:T(8,128)(2,1)}), bf16[1024,1536]{1,0:T(8,128)(2,1)}) %all-gather.10.cloned.1.call-update) | async-done | bytes 3145744 | tf_op jit(solution)/shard_map/all_gather | solution.py:137
  153.7 9.8 fusion.102
  169.1 6.1 squeeze.40
  178.4 6.0 squeeze.39
  198.4 53.6 %while.30 = (s32[]{:T(128)}, bf16[4,512,8,64]{1,3,2,0:T(8,128)(2,1)}, f32[4,8,512]{2,1,0:T(8,128)}, bf16[4,512,8,64]{1,3,2,0:T(8,128)(2,1)}, s32[4]{0:T(128)S(1)...) while((s32[]{:T(128)}, ...), condition=%wide.region_7.8_spmd.clone.clone, body=%wide.region_4.7_spmd.clone.sunk.clone | while | flops 575664640 | bytes 49942764 | solution.py:158
  257.9 7.5 fusion.103
  266.0 97.4 %reduce-scatter.9.cloned.1.call-done = f32[2048,512]{1,0:T(8,128)} async-done(((f32[2048,1024]{1,0:T(8,128)}), f32[2048,512]{1,0:T(8,128)}) %reduce-scatter.9.cloned.1.call-update) | async-done | bytes 4194320 | tf_op jit(solution)/shard_map/reduce_scatter | solution.py:160
  363.4 5.9 fusion.93
  369.3 6.9 all-reduce.3
  382.5 77.0 %collective-permute-done = bf16[1,2048,256]{1,2,0:T(8,128)(2,1)} collective-permute-done((bf16[1,2048,256]{1,2,0:T(8,128)(2,1)S(1)}, bf16[1,2048,256]{1,2,0:T(8,128)(2,1)}, u32[]{:S(2)}, u32[]{:S(2)}) %collective-permute-start) | collective-permute-done | bytes 1048608 | tf_op jit(solution)/shard_map/ppermute | solution.py:24
  472.0 83.2 %collective-permute-done.1 = bf16[2,2048,256]{1,2,0:T(8,128)(2,1)} collective-permute-done((bf16[2,2048,256]{1,2,0:T(8,128)(2,1)}, bf16[2,2048,256]{1,2,0:T(8,128)(2,1)}, u32[]{:S(2)}, u32[]{:S(2)}) %collective-permute-start.1) | collective-permute-done | bytes 2097184 | tf_op jit(solution)/shard_map/ppermute | solution.py:24
  559.5 29.2 %multiply_convert_fusion.1 = (bf16[2048,2048]{1,0:T(8,128)(2,1)}, f32[2048,2048]{1,0:T(8,128)}) fusion(f32[2048]{0:T(1024)S(1)} %copy-done.35, bf16[2048,1024]{1,0:T(8,128)(2,1)} %all-gather.14.cloned.1.call-done, bf16[1024,2048]{1,0:T(8,128)(2,1)} %all-gather.16.cloned.1.call-done), kind=kOutput, calls=%fused_computation.79 | convolution fusion | flops 8631877632 | bytes 33562624 | tf_op jit(solution)/shard_map/dot_general | solution.py:169
  588.7 24.0 %fusion.101 = (f32[2048]{0:T(1024)}, bf16[2048,2048]{1,0:T(8,128)(2,1)S(1)}) fusion(f32[2048,2048]{1,0:T(8,128)} %get-tuple-element.320, f32[2048]{0:T(1024)S(1)} %copy-done.35, bf16[2048,1024]{1,0:T(8,128)(2,1)} %all-gather.18.cloned.1.call-done, bf16[2048,1024]{0,1:T(8,128)(2,1)} %bitcast.239), kind=kOutput, calls=%fused_computation.152 | convolution fusion | flops 8682207232 | bytes 33570816 | tf_op jit(solution)/shard_map/td,fd->tf/dot_general | solution.py:183
  615.9 10.7 fusion.87
  626.8 13.9 %convolution_convert_fusion.2 = bf16[2048,1024]{1,0:T(8,128)(2,1)} fusion(bf16[2048,2048]{1,0:T(8,128)(2,1)} %get-tuple-element.319, bf16[2048,1024]{0,1:T(8,128)(2,1)} %bitcast.240), kind=kOutput, calls=%fused_computation.128 | convolution fusion | flops 8592031744 | bytes 16777216 | tf_op jit(solution)/shard_map/dot_general | solution.py:172
  640.7 39.7 %reduce-scatter.13.cloned.1.call-done = bf16[2048,512]{1,0:T(8,128)(2,1)} async-done(((bf16[2048,1024]{1,0:T(8,128)(2,1)}), bf16[2048,512]{1,0:T(8,128)(2,1)}) %reduce-scatter.13.cloned.1.call-update) | async-done | bytes 2097168 | tf_op jit(solution)/shard_map/reduce_scatter | solution.py:57
  685.3 6.9 all-reduce.2
  692.2 45.0 %reduce-scatter.11.cloned.1.call-done = bf16[2048,512]{1,0:T(8,128)(2,1)} async-done(((bf16[2048,1024]{1,0:T(8,128)(2,1)}), bf16[2048,512]{1,0:T(8,128)(2,1)}) %reduce-scatter.11.cloned.1.call-update) | async-done | bytes 2097168 | tf_op jit(solution)/shard_map/reduce_scatter | solution.py:175
  737.2 8.2 fusion.94
  748.9 14.5 %convolution_convert_fusion.3 = bf16[2048,1024]{1,0:T(8,128)(2,1)} fusion(bf16[2048,2048]{1,0:T(8,128)(2,1)} %get-tuple-element.319, bf16[2048,1024]{1,0:T(8,128)(2,1)} %all-gather.18.cloned.1.call-done), kind=kOutput, calls=%fused_computation.129 | convolution fusion | flops 8592031744 | bytes 16777216 | tf_op jit(solution)/shard_map/tf,td->fd/dot_general | solution.py:182
  763.5 14.0 %fusion.90 = bf16[1024,2048]{1,0:T(8,128)(2,1)} fusion(bf16[2048,1024]{1,0:T(8,128)(2,1)} %all-gather.14.cloned.1.call-done, bf16[2048,2048]{1,0:T(8,128)(2,1)} %copy-done.38), kind=kOutput, calls=%fused_computation.127 | convolution fusion | flops 8592031744 | bytes 16777216 | tf_op jit(solution)/shard_map/td,tf->df/dot_general | solution.py:186
  777.6 28.3 %all-gather.20.cloned.1.call-done = bf16[2048,1024]{1,0:T(8,128)(2,1)} async-done(((bf16[2048,512]{1,0:T(8,128)(2,1)}), bf16[2048,1024]{1,0:T(8,128)(2,1)}) %all-gather.20.cloned.1.call-update) | async-done | bytes 4194320 | tf_op jit(solution)/shard_map/all_gather | solution.py:192
  819.0 6.1 convolution_convert_fusion.5
  825.1 133.3 %while.31 = (s32[]{:T(128)}, f32[4,512,8,64]{1,3,2,0:T(8,128)}, bf16[4,512,8,64]{1,3,2,0:T(8,128)(2,1)}, f32[4,512,8,64]{1,3,2,0:T(8,128)}, bf16[4,512,8,64]{1,3...) while((s32[]{:T(128)}, f32[4,512,8,64]{1,3,2,0:T(8,128)}, ...), condition=%wide.region_21.22_spmd.clone.clone, body=%wide.region_19.21_spmd.clone.sunk.clone | while | flops 1366815232 | bytes 122771752 | solution.py:198
  829.7 8.9 multiply_reduce_fusion.4
  838.7 8.1 multiply_convert_fusion.4
  846.8 6.0 fusion.183
  863.0 8.9 multiply_reduce_fusion.4
  872.0 8.1 multiply_convert_fusion.4
  880.1 5.9 fusion.183
  896.4 8.9 multiply_reduce_fusion.4
  905.3 8.1 multiply_convert_fusion.4
  913.5 6.0 fusion.183
  929.7 8.9 multiply_reduce_fusion.4
  938.6 8.1 multiply_convert_fusion.4
  946.8 6.0 fusion.183
  958.7 7.1 fusion.98
  966.5 8.3 copy.59
  974.9 5.6 copy.72
  983.2 8.5 convolution_convert_fusion
  995.2 61.7 %reduce-scatter.17.cloned.1.call-done = bf16[256,1536]{1,0:T(8,128)(2,1)} async-done(((bf16[1024,1536]{1,0:T(8,128)(2,1)}), bf16[256,1536]{1,0:T(8,128)(2,1)}) %reduce-scatter.17.cloned.1.call-update) | async-done | bytes 786448 | tf_op jit(solution)/shard_map/reduce_scatter | solution.py:232
  1056.9 11.7 convolution_convert_fusion.1
  1076.7 51.6 %all-reduce.8.cloned.1.call-done = (bf16[256,1536]{1,0:T(8,128)(2,1)}, bf16[512,256]{1,0:T(8,128)(2,1)}, bf16[256,2048]{1,0:T(8,128)(2,1)}, bf16[2048,256]{1,0:T(8,128)(2,1)}) async-done(((bf16[256,1536]{1,0:T(8,128)(2,1)}, bf16[512,256]{1,0:T(8,128)(2,1)}, bf16[256,2048]{1,0:T(8,128)(2,1)}, bf16[2048,256]{1,0:T(8,128)(2,1)}), (bf16[256,1536]{1,0:T(8,128)(2,1)}, bf16[512,256]{1,0:T(8,128)(2,1)}, ...) | async-done | bytes 3145744 | tf_op jit(solution)/shard_map/psum | solution.py:226
  1137.0 47.9 %reduce-scatter.15.cloned.1.call-done = bf16[2048,512]{1,0:T(8,128)(2,1)} async-done(((bf16[2048,1024]{1,0:T(8,128)(2,1)}), bf16[2048,512]{1,0:T(8,128)(2,1)}) %reduce-scatter.15.cloned.1.call-update) | async-done | bytes 2097168 | tf_op jit(solution)/shard_map/reduce_scatter | solution.py:57
  1189.2 6.9 all-reduce.1
  1207.1 59.9 %all-reduce = (f32[512]{0:T(512)}, f32[512]{0:T(512)}, f32[512]{0:T(512)}, f32[512]{0:T(512)}, f32[512]{0:T(512)}, /*index=5*/f32[512]{0:T(512)}, f32[512]{0:T(512)}, f32[2048]{0:T(1024)}, f32[512]{0:T(512)}) all-reduce(f32[512]{0:T(512)S(1)} %get-tuple-element.228, ...), channel_id=1, replica_groups=mesh['dp'=4,'row'=4,'col'=2] {'dp','row'}, use_global_device_ids=true, to_apply=%region_28.29 | all-reduce | flops 6144 | bytes 49152 | tf_op jit(solution)/shard_map/psum | solution.py:210
  (272 shorter events, 228.3 us)
Async XLA Ops:
  7.2 81.4 %all-gather.8.cloned.1.call-start = ((), (), s32[]{:S(2)}) async-start(), calls=%async_computation.8 | async-start | bytes 6291456 | tf_op jit(solution)/shard_map/all_gather | solution.py:53
  12.6 15.2 %copy-start.20 = (f32[512]{0:T(512)S(1)}, f32[512]{0:T(512)}, u32[]{:S(2)}) copy-start(f32[512]{0:T(512)} %param.22) | copy-start | bytes 6148
  12.6 15.2 %copy-start.26 = (f32[512]{0:T(512)S(1)}, f32[512]{0:T(512)}, u32[]{:S(2)}) copy-start(f32[512]{0:T(512)} %param.23) | copy-start | bytes 6148
  31.4 122.2 %all-gather.10.cloned.1.call-start = ((), (), s32[]{:S(2)}) async-start(), calls=%async_computation.9 | async-start | bytes 3932160 | tf_op jit(solution)/shard_map/all_gather | solution.py:137
  32.2 225.7 %all-gather.12.cloned.1.call-start = ((), (), s32[]{:S(2)}) async-start(), calls=%async_computation.10 | async-start | bytes 1310720 | tf_op jit(solution)/shard_map/all_gather | solution.py:139
  32.9 330.5 %reduce-scatter.9.cloned.1.call-start = ((), (), s32[]{:S(2)}) async-start(), calls=%async_computation.11 | async-start | bytes 12582912 | tf_op jit(solution)/shard_map/reduce_scatter | solution.py:160
  33.2 130.3 %copy-start.3 = (bf16[4,512,8,64]{1,3,2,0:T(8,128)(2,1)}, bf16[4,512,8,64]{1,3,2,0:T(8,128)(2,1)S(1)}, u32[]{:S(2)}) copy-start(bf16[4,512,8,64]{1,3,2,0:T(8,128)(2,1)S(1)} %fusion.100) | copy-start | bytes 6291460
  190.5 7.9 copy-start.36
  252.0 5.9 copy-start.2
  265.3 98.1 %copy-start.31 = (f32[512]{0:T(512)S(1)}, f32[512]{0:T(512)}, u32[]{:S(2)}) copy-start(f32[512]{0:T(512)} %param.28) | copy-start | bytes 6148
  265.4 294.1 %all-gather.16.cloned.1.call-start = ((), (), s32[]{:S(2)}) async-start(), calls=%async_computation.13 | async-start | bytes 5242880 | tf_op jit(solution)/shard_map/all_gather | solution.py:138
  266.0 110.3 %copy-start.19 = (f32[512]{0:T(512)S(1)}, f32[512]{0:T(512)}, u32[]{:S(2)}) copy-start(f32[512]{0:T(512)} %param.29) | copy-start | bytes 6148
  266.0 110.3 %copy-start.27 = (f32[512]{0:T(512)S(1)}, f32[512]{0:T(512)}, u32[]{:S(2)}) copy-start(f32[512]{0:T(512)} %param.30) | copy-start | bytes 6148
  266.0 293.5 %all-gather.14.cloned.1.call-start = ((), (), s32[]{:S(2)}) async-start(), calls=%async_computation.12 | async-start | bytes 6291456 | tf_op jit(solution)/shard_map/all_gather | solution.py:53
  380.0 208.7 %all-gather.18.cloned.1.call-start = ((), (), s32[]{:S(2)}) async-start(), calls=%async_computation.15 | async-start | bytes 6291456 | tf_op jit(solution)/shard_map/all_gather | solution.py:181
  380.7 78.8 %collective-permute-start = (bf16[1,2048,256]{1,2,0:T(8,128)(2,1)S(1)}, bf16[1,2048,256]{1,2,0:T(8,128)(2,1)}, u32[]{:S(2)}, u32[]{:S(2)}) collective-permute-start(bf16[1,2048,256]{1,2,0:T(8,128)(2,1)S(1)} %bitcast.238), channel_id=1, source_target_pairs={{0,2},{2,0},{4,6},{6,4},{1,3},{3,1},{5,7},{7,5},{8,10},{10,8},{12,... | collective-permute-start | bytes 3145736 | tf_op jit(solution)/shard_map/ppermute | solution.py:24
  462.4 92.8 %collective-permute-start.1 = (bf16[2,2048,256]{1,2,0:T(8,128)(2,1)}, bf16[2,2048,256]{1,2,0:T(8,128)(2,1)}, u32[]{:S(2)}, u32[]{:S(2)}) collective-permute-start(bf16[2,2048,256]{1,2,0:T(8,128)(2,1)} %pad_maximum_fusion.2), channel_id=1, source_target_pairs={{0,4},{2,6},{4,0},{6,2},{1,5},{3,7},{5,1},{7,3},{8,12},{10,14},{12... | collective-permute-start | bytes 6291464 | tf_op jit(solution)/shard_map/ppermute | solution.py:24
  472.0 208.5 %reduce-scatter.13.cloned.1.call-start = ((), (), s32[]{:S(2)}) async-start(), calls=%async_computation.16 | async-start | bytes 6291456 | tf_op jit(solution)/shard_map/reduce_scatter | solution.py:57
  588.7 27.2 %copy-start.33 = (bf16[1024,2048]{1,0:T(8,128)(2,1)S(1)}, bf16[1024,2048]{1,0:T(8,128)(2,1)}, u32[]{:S(2)}) copy-start(bf16[1024,2048]{1,0:T(8,128)(2,1)} %all-gather.16.cloned.1.call-done) | copy-start | bytes 12582916
  626.7 110.4 %reduce-scatter.11.cloned.1.call-start = ((), (), s32[]{:S(2)}) async-start(), calls=%async_computation.14 | async-start | bytes 6291456 | tf_op jit(solution)/shard_map/reduce_scatter | solution.py:175
  640.7 96.5 %copy-start.28 = (f32[512]{0:T(512)S(1)}, f32[512]{0:T(512)}, u32[]{:S(2)}) copy-start(f32[512]{0:T(512)} %param.34) | copy-start | bytes 6148
  640.7 165.2 %all-gather.20.cloned.1.call-start = ((), (), s32[]{:S(2)}) async-start(), calls=%async_computation.17 | async-start | bytes 6291456 | tf_op jit(solution)/shard_map/all_gather | solution.py:192
  680.4 56.7 %copy-start.7 = (bf16[2048,512]{1,0:T(8,128)(2,1)S(1)}, bf16[2048,512]{1,0:T(8,128)(2,1)}, u32[]{:S(2)}) copy-start(bf16[2048,512]{1,0:T(8,128)(2,1)} %reduce-scatter.13.cloned.1.call-done) | copy-start | bytes 6291460
  748.9 242.8 %reduce-scatter.23.cloned.1.call-start = ((), (), s32[]{:S(2)}) async-start(), calls=%async_computation.22 | async-start | bytes 5242880 | tf_op jit(solution)/shard_map/reduce_scatter | solution.py:241
  763.4 228.3 %reduce-scatter.21.cloned.1.call-start = ((), (), s32[]{:S(2)}) async-start(), calls=%async_computation.21 | async-start | bytes 5242880 | tf_op jit(solution)/shard_map/reduce_scatter | solution.py:235
  777.5 28.4 %copy-start.34 = (bf16[512,1024]{1,0:T(8,128)(2,1)S(1)}, bf16[512,1024]{1,0:T(8,128)(2,1)}, u32[]{:S(2)}) copy-start(bf16[512,1024]{1,0:T(8,128)(2,1)} %all-gather.12.cloned.1.call-done) | copy-start | bytes 3145732
  777.6 217.6 %reduce-scatter.19.cloned.1.call-start = ((), (), s32[]{:S(2)}) async-start(), calls=%async_computation.20 | async-start | bytes 1310720 | tf_op jit(solution)/shard_map/reduce_scatter | solution.py:238
  819.0 6.1 copy-start.37
  829.7 8.9 copy-start
  846.8 6.0 copy-start.4
  863.0 8.9 copy-start
  880.1 5.9 copy-start.4
  896.4 8.9 copy-start
  913.5 6.0 copy-start.4
  929.7 8.9 copy-start
  946.8 6.0 copy-start.4
  958.5 98.4 %reduce-scatter.17.cloned.1.call-start = ((), (), s32[]{:S(2)}) async-start(), calls=%async_computation.19 | async-start | bytes 3932160 | tf_op jit(solution)/shard_map/reduce_scatter | solution.py:232
  958.7 7.1 copy-start.6
  974.9 8.3 copy-start.32
  991.7 136.7 %all-reduce.8.cloned.1.call-start = ((), (), s32[]{:S(2)}) async-start(), calls=%async_computation.23 | async-start | bytes 6291456 | tf_op jit(solution)/shard_map/psum | solution.py:226
  1056.9 128.0 %reduce-scatter.15.cloned.1.call-start = ((), (), s32[]{:S(2)}) async-start(), calls=%async_computation.18 | async-start | bytes 6291456 | tf_op jit(solution)/shard_map/reduce_scatter | solution.py:57
  1128.3 7.2 copy-start.13
  1130.2 54.7 %copy-start.16 = (f32[2048]{0:T(1024)S(1)}, f32[2048]{0:T(1024)}, u32[]{:S(2)}) copy-start(f32[2048]{0:T(1024)} %copy-done.15) | copy-start | bytes 24580
  1130.2 54.7 %copy-start.18 = (f32[2048]{0:T(1024)S(1)}, f32[2048]{0:T(1024)}, u32[]{:S(2)}) copy-start(f32[2048]{0:T(1024)} %copy-done.17) | copy-start | bytes 24580
  1130.2 54.7 %copy-start.21 = (f32[512]{0:T(512)S(1)}, f32[512]{0:T(512)}, u32[]{:S(2)}) copy-start(f32[512]{0:T(512)} %param.22) | copy-start | bytes 6148
  1184.9 11.2 copy-start.8
  1201.7 5.4 copy-start.24
  1201.7 5.4 copy-start.25
  (24 other events, 62.2 us)
Sparse Core Ops, SparseCore 0:
  31.5 56.9 all-gather.7
  90.1 63.4 all-gather.9
  155.2 28.8 all-gather.11
  265.5 97.8 reduce-scatter.8
  364.9 101.6 all-gather.15
  468.0 59.2 all-gather.13
  529.0 56.7 all-gather.17
  626.8 53.5 reduce-scatter.12
  682.7 54.3 reduce-scatter.10
  749.0 56.8 all-gather.19
  808.3 76.7 reduce-scatter.22
  887.2 77.2 reduce-scatter.20
  967.5 27.6 reduce-scatter.18
  997.9 58.8 reduce-scatter.16
  1059.3 68.9 all-reduce.7
  1130.5 54.3 reduce-scatter.14
